TPU v7x, 32 devices: a whole 2x2x4 slice. The times are simulated.
32 devices in a mesh: lat: 4 (over y, x), kpt: 8 (over z, core).
Axes of the slice: x: 2, y: 2, z: 4, core: 2. Of those that a mesh axis runs over, the one named last changes fastest.
Arguments:
- coarse: bfloat16 [2, 4, 32, 12288], P(None, 'lat', 'kpt'), may hold values from -1 to 1
- rp_vectors: int32 [4, 3], P('lat'), may hold values from -4 to 4
- rp_weights: int32 [4], P('lat'), may hold values from 1 to 3
- re_vectors: int32 [32, 3], replicated, may hold values from -4 to 4
- re_weights: int32 [32], replicated, may hold values from 1 to 3
- q_points: float32 [2, 3], replicated, may hold values from 0 to 1
- k_points: float32 [512, 3], P('kpt'), may hold values from 0 to 1
- modes_rot: bfloat16 [2, 2, 48, 48], replicated, may hold values from -0.625 to 0.625
- u_k: bfloat16 [2, 512, 16, 16], P(None, 'kpt'), may hold values from -1 to 1
- u_kq: bfloat16 [2, 2, 512, 16, 16], P(None, None, 'kpt'), may hold values from -1 to 1
- mask_k: int32 [512, 16], P('kpt'), may hold values 0 or 1
- mask_kq: int32 [2, 512, 16], P(None, 'kpt'), may hold values 0 or 1
Outputs:
- coupling: bfloat16 [2, 512, 2, 12288], P(None, 'kpt', None, 'lat')
All inputs are finite; a program needn't handle non-finite values. No bound on the sum of `mask_k` or of `mask_kq` on one device may be relied on, other than what follows from the above.
Results may differ from a plain program's by a relative error of at most 0.017.
Values may be sent and summed in bfloat16 or wider, within the bound.
A program may use at most 128 MiB of HBM per device.

v0:
```python
import jax
import jax.numpy as jnp
from jax import lax
from jax.sharding import PartitionSpec as P

two_pi = 6.283185307179586


def phases(points, vectors, weights):
    cells = vectors.astype(jnp.float32)
    argument = two_pi * (
        points[:, 0:1] * cells[None, :, 0]
        + points[:, 1:2] * cells[None, :, 1]
        + points[:, 2:3] * cells[None, :, 2]
    )
    inverse = 1.0 / weights.astype(jnp.float32)
    return (
        (jnp.cos(argument) * inverse).astype(jnp.bfloat16),
        (jnp.sin(argument) * inverse).astype(jnp.bfloat16),
    )


def rotate_modes(values, modes_rot):
    shape = values.shape
    mode_count = modes_rot.shape[2]
    split = values.reshape(shape[0], shape[1], shape[2], mode_count, shape[3] // mode_count)
    br = jnp.einsum(
        "qmn,qrmx->qrnx", modes_rot[0], split[0], preferred_element_type=jnp.float32
    ) - jnp.einsum("qmn,qrmx->qrnx", modes_rot[1], split[1], preferred_element_type=jnp.float32)
    bi = jnp.einsum(
        "qmn,qrmx->qrnx", modes_rot[0], split[1], preferred_element_type=jnp.float32
    ) + jnp.einsum("qmn,qrmx->qrnx", modes_rot[1], split[0], preferred_element_type=jnp.float32)
    return jnp.stack([br, bi]).reshape(shape).astype(jnp.bfloat16)


def phonon_sum(block, vectors, weights, q_points):
    phase_real, phase_imag = phases(q_points, vectors, weights)
    rows = block.shape[1]
    cells = block.shape[2]
    lanes = block.shape[3]
    flat_real = block[0].reshape(rows, cells * lanes)
    flat_imag = block[1].reshape(rows, cells * lanes)
    part_real = jnp.dot(phase_real, flat_real, preferred_element_type=jnp.float32) - jnp.dot(
        phase_imag, flat_imag, preferred_element_type=jnp.float32
    )
    part_imag = jnp.dot(phase_real, flat_imag, preferred_element_type=jnp.float32) + jnp.dot(
        phase_imag, flat_real, preferred_element_type=jnp.float32
    )
    return jnp.stack([part_real, part_imag]).reshape(2, q_points.shape[0], cells, lanes)


def per_device(
    coarse,
    rp_vectors,
    rp_weights,
    re_vectors,
    re_weights,
    q_points,
    k_points,
    modes_rot,
    u_k,
    u_kq,
    mask_k,
    mask_kq,
):
    q_count = q_points.shape[0]
    k_count = k_points.shape[0]
    band_count = u_k.shape[2]
    all_vectors, all_weights = (
        lax.all_gather(rp_vectors, "lat", axis=0, tiled=True),
        lax.all_gather(rp_weights, "lat", axis=0, tiled=True),
    )
    blocks = lax.all_to_all(coarse, "lat", split_axis=2, concat_axis=1, tiled=True)
    summed = phonon_sum(blocks, all_vectors, all_weights, q_points).astype(jnp.bfloat16)
    rotated = rotate_modes(summed, modes_rot)
    shared = lax.all_to_all(rotated, "lat", split_axis=3, concat_axis=2, tiled=True)
    lane_local = shared.shape[3]
    portion = lax.all_gather(shared, "kpt", axis=2, tiled=True)
    kreal, kimag = phases(k_points, re_vectors, re_weights)
    er = jnp.einsum(
        "kr,qrx->kqx", kreal, portion[0], preferred_element_type=jnp.float32
    ) - jnp.einsum("kr,qrx->kqx", kimag, portion[1], preferred_element_type=jnp.float32)
    ei = jnp.einsum(
        "kr,qrx->kqx", kreal, portion[1], preferred_element_type=jnp.float32
    ) + jnp.einsum("kr,qrx->kqx", kimag, portion[0], preferred_element_type=jnp.float32)
    totals = jnp.stack([er, ei])
    mode_local = lane_local // (band_count * band_count)
    field = totals.astype(jnp.bfloat16).reshape(
        2, k_count, q_count, mode_local, band_count, band_count
    )
    tr = jnp.einsum(
        "kqmab,kbn->kqman", field[0], u_k[0], preferred_element_type=jnp.float32
    ) - jnp.einsum("kqmab,kbn->kqman", field[1], u_k[1], preferred_element_type=jnp.float32)
    ti = jnp.einsum(
        "kqmab,kbn->kqman", field[0], u_k[1], preferred_element_type=jnp.float32
    ) + jnp.einsum("kqmab,kbn->kqman", field[1], u_k[0], preferred_element_type=jnp.float32)
    tr = tr.astype(jnp.bfloat16)
    ti = ti.astype(jnp.bfloat16)
    outr = jnp.einsum(
        "qkac,kqman->kqmcn", u_kq[0], tr, preferred_element_type=jnp.float32
    ) + jnp.einsum("qkac,kqman->kqmcn", u_kq[1], ti, preferred_element_type=jnp.float32)
    outi = jnp.einsum(
        "qkac,kqman->kqmcn", u_kq[0], ti, preferred_element_type=jnp.float32
    ) - jnp.einsum("qkac,kqman->kqmcn", u_kq[1], tr, preferred_element_type=jnp.float32)
    window = (
        jnp.transpose(mask_kq.astype(jnp.float32), (1, 0, 2))[:, :, None, :, None]
        * mask_k.astype(jnp.float32)[:, None, None, None, :]
    )
    result = jnp.stack([outr * window, outi * window])
    return result.reshape(2, k_count, q_count, lane_local).astype(jnp.bfloat16)


def solution(mesh):
    placed = (
        P(None, "lat", "kpt", None),
        P("lat", None),
        P("lat"),
        P(),
        P(),
        P(),
        P("kpt", None),
        P(),
        P(None, "kpt", None, None),
        P(None, None, "kpt", None, None),
        P("kpt", None),
        P(None, "kpt", None),
    )
    return jax.shard_map(
        per_device,
        mesh=mesh,
        in_specs=placed,
        out_specs=P(None, "kpt", None, "lat"),
        check_vma=False,
    )
```

profile of v0, /device:TPU:0, one launch (start us, length us, event | category | flops | bytes accessed | tf_op | source)
XLA Modules:
  0.0 252.8 jit_solution(12334398810767427954)
XLA Ops:
  0.7 1.8 copy.132
  2.5 1.2 dynamic-slice
  4.4 5.2 %all-to-all-start = ((bf16[2,1,4,12288]{3,0,1,2:T(2,128)(2,1)}), bf16[2,1,4,12288]{3,0,1,2:T(2,128)(2,1)S(1)}, u32[]{:S(2)}, u32[]{:S(2)}) async-start(bf16[2,1,4,12288]{3,0,1,2:T(2,128)(2,1)} %copy.132), calls=%async_computation | async-start | bytes 393216 | tf_op jit(solution)/shard_map/all_to_all | solution.py:73
  9.6 7.9 %all-reduce = s32[4]{0:T(128)S(1)} all-reduce(s32[4]{0:T(128)S(1)} %dynamic-update-slice), channel_id=1, replica_groups=mesh['lat'=4,'kpt'=8] {'lat'}, use_global_device_ids=true, to_apply=%add | all-reduce | flops 4 | bytes 32
  17.5 1.0 slice_reduce_fusion.5
  18.5 0.8 slice_bitcast_fusion.5
  19.3 7.8 %all-gather = s32[4,1,3]{2,1,0:T(1,128)S(1)} all-gather(s32[1,1,3]{2,1,0:T(1,128)} %bitcast.155), channel_id=1, replica_groups=mesh['lat'=4,'kpt'=8] {'lat'}, dimensions={0}, use_global_device_ids=true | all-gather | bytes 60 | tf_op jit(solution)/shard_map/all_gather | solution.py:70
  27.3 0.7 convert_element_type.56
  28.0 0.7 convert_element_type.67
  28.7 0.7 convert_bitcast_fusion
  29.4 0.9 fusion.67
  30.3 1.0 fusion.65
  31.3 0.7 broadcast_multiply_fusion
  33.4 0.9 fusion.35
  34.3 0.9 fusion.33
  35.3 0.9 fusion.9
  36.2 0.9 fusion.8
  37.3 10.0 %copy.135 = bf16[2,2,1,12288]{1,0,2,3:T(2,128)(2,1)} copy(bf16[2,2,1,12288]{3,1,2,0:T(2,128)(2,1)S(1)} %pad_maximum_fusion.1) | data formatting | bytes 196608 | tf_op jit(solution)/shard_map/stack | solution.py:33
  47.3 11.9 %reshape.167 = bf16[4,2,6144]{2,1,0:T(2,128)(2,1)} reshape(bf16[12288,1,2,2]{3,2,1,0:T(2,128)(2,1)} %bitcast.144) | data formatting | bytes 196608
  59.3 3.3 %all-to-all-start.1 = ((bf16[4,2,6144]{2,1,0:T(2,128)(2,1)}), bf16[4,2,6144]{2,1,0:T(2,128)(2,1)S(1)}, u32[]{:S(2)}, u32[]{:S(2)}) async-start(bf16[4,2,6144]{2,1,0:T(2,128)(2,1)} %reshape.167), calls=%async_computation.1 | async-start | bytes 196608 | tf_op jit(solution)/shard_map/all_to_all | solution.py:76
  62.9 0.9 copy.176
  63.8 0.8 copy.178
  64.6 0.8 copy.177
  65.4 2.1 all-to-all-done.1
  67.5 14.7 %reshape.168 = bf16[12288,1,2,2]{3,2,1,0:T(2,128)(2,1)} reshape(bf16[4,2,6144]{2,1,0:T(2,128)(2,1)S(1)} %all-to-all-done.1) | data formatting | bytes 196608
  82.2 12.7 %copy.137 = bf16[2,2,4,3072]{3,1,0,2:T(2,128)(2,1)S(1)} copy(bf16[2,2,4,3072]{1,0,3,2:T(2,128)(2,1)} %bitcast.145) | data formatting | bytes 196608 | tf_op jit(solution)/shard_map/all_to_all | solution.py:76
  94.8 16.5 %all_gather.11 = bf16[2,2,32,3072]{3,1,0,2:T(2,128)(2,1)S(1)} all-gather(bf16[2,2,4,3072]{3,1,0,2:T(2,128)(2,1)S(1)} %copy.137), channel_id=1, replica_groups=mesh['lat'=4,'kpt'=8] {'kpt'}, dimensions={2}, use_global_device_ids=true | all-gather | bytes 884736 | tf_op jit(solution)/shard_map/all_gather | solution.py:78
  112.9 1.4 fusion.3
  114.4 2.4 copy.143
  116.8 1.4 fusion.2
  118.2 1.8 copy.140
  120.0 9.8 %copy.142 = bf16[64,2,12,16,16]{4,3,2,1,0:T(8,128)(2,1)} copy(bf16[64,2,12,16,16]{0,4,3,2,1:T(8,128)(2,1)S(1)} %bitcast.147) | data formatting | bytes 1572864 | tf_op jit(solution)/shard_map/squeeze | solution.py:92
  129.8 10.8 %copy.145 = bf16[64,2,12,16,16]{4,3,2,1,0:T(8,128)(2,1)} copy(bf16[64,2,12,16,16]{0,4,3,2,1:T(8,128)(2,1)} %bitcast.146) | data formatting | bytes 1572864 | tf_op jit(solution)/shard_map/squeeze | solution.py:93
  140.6 9.2 %fusion.23 = f32[64,2,12,16,16]{4,3,2,1,0:T(8,128)} fusion(bf16[64,2,12,16,16]{4,3,2,1,0:T(8,128)(2,1)} %copy.142, bf16[1,64,16,16]{3,2,1,0:T(8,128)(2,1)} %copy.176), kind=kOutput, calls=%fused_computation.36 | convolution fusion | flops 12582912 | bytes 2392064 | tf_op jit(solution)/shard_map/kqmab,kbn->kqman/dot_general | solution.py:94
  149.8 5.5 %fusion.21 = f32[64,2,12,16,16]{4,3,2,1,0:T(8,128)} fusion(bf16[64,2,12,16,16]{4,3,2,1,0:T(8,128)(2,1)S(1)} %bitcast.143, bf16[1,64,16,16]{3,2,1,0:T(8,128)(2,1)S(1)} %copy.175), kind=kOutput, calls=%fused_computation.34 | convolution fusion | flops 12582912 | bytes 2392064 | tf_op jit(solution)/shard_map/kqmab,kbn->kqman/dot_general | solution.py:91
  155.3 8.2 %add_convert_fusion = bf16[64,2,12,16,16]{4,3,2,1,0:T(8,128)(2,1)S(1)} fusion(f32[64,2,12,16,16]{4,3,2,1,0:T(8,128)} %fusion.23, bf16[64,2,12,16,16]{4,3,2,1,0:T(8,128)(2,1)} %copy.145, bf16[1,64,16,16]{3,2,1,0:T(8,128)(2,1)S(1)} %copy.175), kind=kOutput, calls=%fused_computation.4 | convolution fusion | flops 13369344 | bytes 3178496 | tf_op jit(solution)/shard_map/kqmab,kbn->kqman/dot_general | solution.py:96
  163.5 10.9 %subtract_convert_fusion = bf16[64,2,12,16,16]{4,3,2,1,0:T(8,128)(2,1)} fusion(f32[64,2,12,16,16]{4,3,2,1,0:T(8,128)} %fusion.21, bf16[64,2,12,16,16]{4,3,2,1,0:T(8,128)(2,1)} %copy.145, bf16[1,64,16,16]{3,2,1,0:T(8,128)(2,1)S(1)} %copy-done.1), kind=kOutput, calls=%fused_computation.5 | convolution fusion | flops 13369344 | bytes 3178496 | tf_op jit(solution)/shard_map/kqmab,kbn->kqman/dot_general | solution.py:93
  174.4 9.7 %fusion.10 = f32[64,2,12,16,16]{4,3,2,1,0:T(8,128)} fusion(bf16[64,2,12,16,16]{4,3,2,1,0:T(8,128)(2,1)} %subtract_convert_fusion, bf16[1,2,64,16,16]{4,3,1,2,0:T(8,128)(2,1)S(1)} %copy.178), kind=kOutput, calls=%fused_computation.21 | convolution fusion | flops 12582912 | bytes 2424832 | tf_op jit(solution)/shard_map/qkac,kqman->kqmcn/dot_general | solution.py:104
  184.1 5.7 %fusion.16 = f32[64,2,12,16,16]{4,3,2,1,0:T(8,128)} fusion(bf16[64,2,12,16,16]{4,3,2,1,0:T(8,128)(2,1)S(1)} %copy-done, bf16[1,2,64,16,16]{4,3,1,2,0:T(8,128)(2,1)S(1)} %copy.177), kind=kOutput, calls=%fused_computation.27 | convolution fusion | flops 12582912 | bytes 2424832 | tf_op jit(solution)/shard_map/qkac,kqman->kqmcn/dot_general | solution.py:99
  189.8 5.6 %fusion.14 = f32[64,2,12,16,16]{4,3,2,1,0:T(8,128)} fusion(bf16[64,2,12,16,16]{4,3,2,1,0:T(8,128)(2,1)S(1)} %add_convert_fusion, bf16[1,2,64,16,16]{4,3,1,2,0:T(8,128)(2,1)S(1)} %copy.177), kind=kOutput, calls=%fused_computation.25 | convolution fusion | flops 12582912 | bytes 2424832 | tf_op jit(solution)/shard_map/qkac,kqman->kqmcn/dot_general | solution.py:102
  195.5 5.8 %fusion.12 = f32[64,2,12,16,16]{4,3,2,1,0:T(8,128)} fusion(bf16[64,2,12,16,16]{4,3,2,1,0:T(8,128)(2,1)S(1)} %add_convert_fusion, bf16[1,2,64,16,16]{4,3,1,2,0:T(8,128)(2,1)S(1)} %copy.178), kind=kOutput, calls=%fused_computation.23 | convolution fusion | flops 12582912 | bytes 2424832 | tf_op jit(solution)/shard_map/qkac,kqman->kqmcn/dot_general | solution.py:101
  201.3 9.7 %copy.157 = f32[64,2,12,16,16]{0,3,4,2,1:T(8,128)S(1)} copy(f32[64,2,12,16,16]{4,3,2,1,0:T(8,128)} %fusion.10) | data formatting | bytes 3145728 | tf_op jit(solution)/shard_map/qkac,kqman->kqmcn/dot_general | solution.py:104
  211.0 10.9 %copy.152 = f32[64,2,12,16,16]{0,3,4,2,1:T(8,128)} copy(f32[64,2,12,16,16]{4,3,2,1,0:T(8,128)} %fusion.16) | data formatting | bytes 3145728 | tf_op jit(solution)/shard_map/qkac,kqman->kqmcn/dot_general | solution.py:99
  221.9 10.9 %copy.156 = f32[64,2,12,16,16]{0,3,4,2,1:T(8,128)} copy(f32[64,2,12,16,16]{4,3,2,1,0:T(8,128)} %fusion.14) | data formatting | bytes 3145728 | tf_op jit(solution)/shard_map/qkac,kqman->kqmcn/dot_general | solution.py:102
  232.8 10.9 %copy.153 = f32[64,2,12,16,16]{0,3,4,2,1:T(8,128)} copy(f32[64,2,12,16,16]{4,3,2,1,0:T(8,128)} %fusion.12) | data formatting | bytes 3145728 | tf_op jit(solution)/shard_map/qkac,kqman->kqmcn/dot_general | solution.py:101
  243.7 5.0 %fusion.5 = (bf16[64,2,12,16,16]{0,4,3,2,1:T(8,128)(2,1)S(1)}, bf16[64,2,12,16,16]{0,4,3,2,1:T(8,128)(2,1)S(1)}) fusion(f32[64,2,12,16,16]{0,3,4,2,1:T(8,128)} %copy.152, f32[64,2,12,16,16]{0,3,4,2,1:T(8,128)} %copy.153, f32[64,2,16,16]{0,3,2,1:T(8,128)S(1)} %copy-done.2, f32[64,2,12,16,16]{0,3,4,2,1:T(8,128)} %copy.156, f32[64,2,12,16,16]{0,3,4,2,1:T(8,128)S(1)} %copy.157), kind=kLoop, calls=%fused_computation.14 | loop fusion | flops 2359296 | bytes 7995392 | tf_op jit(solution)/shard_map/convert.3
  248.8 0.7 pad_maximum_fusion
  249.5 3.3 %copy.158 = bf16[2,64,2,3072]{3,2,1,0:T(2,128)(2,1)} copy(bf16[2,64,2,3072]{1,3,2,0:T(8,128)(2,1)S(1)} %pad_maximum_fusion) | data formatting | bytes 3145728 | tf_op jit(solution)/shard_map/stack | solution.py:109
  (34 shorter events, 4.3 us)
Async XLA Ops:
  4.4 27.8 %all-to-all-start = ((bf16[2,1,4,12288]{3,0,1,2:T(2,128)(2,1)}), bf16[2,1,4,12288]{3,0,1,2:T(2,128)(2,1)S(1)}, u32[]{:S(2)}, u32[]{:S(2)}) async-start(bf16[2,1,4,12288]{3,0,1,2:T(2,128)(2,1)} %copy.132), calls=%async_computation | async-start | bytes 393216 | tf_op jit(solution)/shard_map/all_to_all | solution.py:73
  37.3 25.3 %copy-start.3 = (s32[32]{0:T(128)S(1)}, s32[32]{0:T(128)}, u32[]{:S(2)}) copy-start(s32[32]{0:T(128)} %param.16) | copy-start | bytes 388
  59.3 8.2 %all-to-all-start.1 = ((bf16[4,2,6144]{2,1,0:T(2,128)(2,1)}), bf16[4,2,6144]{2,1,0:T(2,128)(2,1)S(1)}, u32[]{:S(2)}, u32[]{:S(2)}) async-start(bf16[4,2,6144]{2,1,0:T(2,128)(2,1)} %reshape.167), calls=%async_computation.1 | async-start | bytes 196608 | tf_op jit(solution)/shard_map/all_to_all | solution.py:76
  129.8 20.0 %slice-start = ((s8[6291456]{0:T(1024)(128)(4,1)}), s8[2097152]{0:T(1024)(128)(4,1)S(1)}, s32[]{:S(2)}) async-start(s8[6291456]{0:T(1024)(128)(4,1)} %bitcast.142), calls=%async_computation.2 | async-start | bytes 4194304
  140.6 9.2 %slice-start.1 = ((s8[6291456]{0:T(1024)(128)(4,1)}), s8[4194304]{0:T(1024)(128)(4,1)S(1)}, s32[]{:S(2)}) async-start(s8[6291456]{0:T(1024)(128)(4,1)} %bitcast.142), calls=%async_computation.3 | async-start | bytes 8388608
  155.3 8.2 %copy-start.1 = (bf16[1,64,16,16]{3,2,1,0:T(8,128)(2,1)S(1)}, bf16[1,64,16,16]{3,2,1,0:T(8,128)(2,1)}, u32[]{:S(2)}) copy-start(bf16[1,64,16,16]{3,2,1,0:T(8,128)(2,1)} %copy.176) | copy-start | bytes 98308
  174.4 9.7 %copy-start = (bf16[64,2,12,16,16]{4,3,2,1,0:T(8,128)(2,1)S(1)}, bf16[64,2,12,16,16]{4,3,2,1,0:T(8,128)(2,1)}, u32[]{:S(2)}) copy-start(bf16[64,2,12,16,16]{4,3,2,1,0:T(8,128)(2,1)} %subtract_convert_fusion) | copy-start | bytes 2359300
  232.8 10.9 %copy-start.2 = (f32[64,2,16,16]{0,3,2,1:T(8,128)S(1)}, f32[64,2,16,16]{0,3,2,1:T(8,128)}, u32[]{:S(2)}) copy-start(f32[64,2,16,16]{0,3,2,1:T(8,128)} %broadcast_multiply_fusion) | copy-start | bytes 393220
where the time goes:
time: 254 us; the launch traced here: 253 us
  local copies, waits for them, and re-layouts  131 us (52%)
  matrix products  69.2 us (27%)
  blocking collectives  32.2 us (13%)
  other arithmetic  8.81 us (3%)
  starting transfers between devices  8.5 us (3%)
    unnamed x22, local copies, waits for them, and re-layouts  33.1 us
    all_gather x1, blocking collectives, per_device(): portion = lax.all_gather(shared, 'kpt', axis=2, tiled=True)  16.5 us
    all_to_all x1, local copies, waits for them, and re-layouts, per_device(): lax.all_to_all(rotated, 'lat', split_axis=3, concat_axis=2, tiled=True)  12.7 us
    dot_general x1, local copies, waits for them, and re-layouts, per_device(): jnp.einsum('qkac,kqman->kqmcn', u_kq[1], ti, preferred_element_type=jnp.f...  10.9 us
    dot_general x1, local copies, waits for them, and re-layouts, per_device(): jnp.einsum('qkac,kqman->kqmcn', u_kq[0], tr, preferred_element_type=jnp.f...  10.9 us
    dot_general x1, local copies, waits for them, and re-layouts, per_device(): jnp.einsum('qkac,kqman->kqmcn', u_kq[0], ti, preferred_element_type=jnp.f...  10.9 us
    dot_general x1, matrix products, per_device(): jnp.einsum('kqmab,kbn->kqman', field[1], u_k[1], preferred_element_type=j...  10.9 us
    squeeze x1, local copies, waits for them, and re-layouts, per_device(): field[1]  10.8 us
  transfers between devices with their start and end apart: 2, of which 1 were waited for; matrix products, arithmetic and copies ran while one was open for 4% of the time, Pallas kernels for 0%

commit v1 on v0

--- a/solution.py
+++ b/solution.py
@@ -75,7 +75,7 @@
     rotated = rotate_modes(summed, modes_rot)
     shared = lax.all_to_all(rotated, "lat", split_axis=3, concat_axis=2, tiled=True)
     lane_local = shared.shape[3]
-    portion = lax.all_gather(shared, "kpt", axis=2, tiled=True)
+    portion = jnp.concatenate(lax.all_gather(shared, "kpt"), axis=2)
     kreal, kimag = phases(k_points, re_vectors, re_weights)
     er = jnp.einsum(
         "kr,qrx->kqx", kreal, portion[0], preferred_element_type=jnp.float32

time: 254 us -> 257 us (1.012)
  local copies, waits for them, and re-layouts: 131 us -> 135 us
    all_gather x0 -> x1, local copies, waits for them, and re-layouts: none -> 14.5 us  [per_device(): portion = jnp.concatenate(lax.all_gather(shared, 'kpt'), axis=2)]
    all_to_all x1 -> x0, local copies, waits for them, and re-layouts: 12.7 us -> none  [per_device(): lax.all_to_all(rotated, 'lat', split_axis=3, concat_axis=2, tiled=True)]
    unnamed x22 -> x24, local copies, waits for them, and re-layouts: 33.1 us -> 34 us
where the time goes in v1:
time: 257 us; the launch traced here: 255 us
  local copies, waits for them, and re-layouts  135 us (53%)
  matrix products  68.4 us (27%)
  blocking collectives  32.2 us (13%)
  other arithmetic  8.8 us (3%)
  starting transfers between devices  8.5 us (3%)
    unnamed x24, local copies, waits for them, and re-layouts  34 us
    all_gather x1, blocking collectives, per_device(): portion = jnp.concatenate(lax.all_gather(shared, 'kpt'), axis=2)  16.5 us
    all_gather x1, local copies, waits for them, and re-layouts, per_device(): portion = jnp.concatenate(lax.all_gather(shared, 'kpt'), axis=2)  14.5 us
    dot_general x1, local copies, waits for them, and re-layouts, per_device(): jnp.einsum('qkac,kqman->kqmcn', u_kq[1], ti, preferred_element_type=jnp.f...  10.9 us
    dot_general x1, local copies, waits for them, and re-layouts, per_device(): jnp.einsum('qkac,kqman->kqmcn', u_kq[0], tr, preferred_element_type=jnp.f...  10.9 us
    dot_general x1, local copies, waits for them, and re-layouts, per_device(): jnp.einsum('qkac,kqman->kqmcn', u_kq[0], ti, preferred_element_type=jnp.f...  10.9 us
    dot_general x1, matrix products, per_device(): jnp.einsum('kqmab,kbn->kqman', field[1], u_k[1], preferred_element_type=j...  10.9 us
    squeeze x1, local copies, waits for them, and re-layouts, per_device(): field[1]  10.7 us
  transfers between devices with their start and end apart: 2, of which 1 were waited for; matrix products, arithmetic and copies ran while one was open for 4% of the time, Pallas kernels for 0%

profile of v1, /device:TPU:0, one launch (start us, length us, event | category | flops | bytes accessed | tf_op | source)
XLA Modules:
  0.0 254.8 jit_solution(788951968877897935)
XLA Ops:
  0.7 1.8 copy.130
  2.5 1.3 dynamic-slice
  3.8 0.8 dynamic-update-slice
  4.6 5.2 %all-to-all-start = ((bf16[2,1,4,12288]{3,0,1,2:T(2,128)(2,1)}), bf16[2,1,4,12288]{3,0,1,2:T(2,128)(2,1)S(1)}, u32[]{:S(2)}, u32[]{:S(2)}) async-start(bf16[2,1,4,12288]{3,0,1,2:T(2,128)(2,1)} %copy.130), calls=%async_computation | async-start | bytes 393216 | tf_op jit(solution)/shard_map/all_to_all | solution.py:73
  9.8 7.9 %all-reduce = s32[4]{0:T(128)S(1)} all-reduce(s32[4]{0:T(128)S(1)} %dynamic-update-slice), channel_id=1, replica_groups=mesh['lat'=4,'kpt'=8] {'lat'}, use_global_device_ids=true, to_apply=%add | all-reduce | flops 4 | bytes 32
  17.7 1.0 slice_reduce_fusion.5
  18.7 0.8 slice_bitcast_fusion.5
  19.5 7.8 %all-gather = s32[4,1,3]{2,1,0:T(1,128)S(1)} all-gather(s32[1,1,3]{2,1,0:T(1,128)} %bitcast.151), channel_id=1, replica_groups=mesh['lat'=4,'kpt'=8] {'lat'}, dimensions={0}, use_global_device_ids=true | all-gather | bytes 60 | tf_op jit(solution)/shard_map/all_gather | solution.py:70
  28.9 0.7 convert_bitcast_fusion
  29.6 0.9 fusion.67
  30.5 1.0 fusion.65
  31.5 0.7 broadcast_multiply_fusion
  33.6 0.9 fusion.33
  34.5 0.9 fusion.31
  35.5 0.9 fusion.9
  36.4 0.9 fusion.8
  37.5 10.0 %copy.133 = bf16[2,2,1,12288]{1,0,2,3:T(2,128)(2,1)} copy(bf16[2,2,1,12288]{3,1,2,0:T(2,128)(2,1)S(1)} %pad_maximum_fusion.1) | data formatting | bytes 196608 | tf_op jit(solution)/shard_map/stack | solution.py:33
  47.5 11.9 %reshape.177 = bf16[4,2,6144]{2,1,0:T(2,128)(2,1)} reshape(bf16[12288,1,2,2]{3,2,1,0:T(2,128)(2,1)} %bitcast.139) | data formatting | bytes 196608
  59.4 3.3 %all-to-all-start.1 = ((bf16[4,2,6144]{2,1,0:T(2,128)(2,1)}), bf16[4,2,6144]{2,1,0:T(2,128)(2,1)S(1)}, u32[]{:S(2)}, u32[]{:S(2)}) async-start(bf16[4,2,6144]{2,1,0:T(2,128)(2,1)} %reshape.177), calls=%async_computation.1 | async-start | bytes 196608 | tf_op jit(solution)/shard_map/all_to_all | solution.py:76
  62.8 0.9 copy.169
  63.7 0.9 copy.170
  64.6 0.8 copy.172
  65.4 0.8 copy.171
  66.2 1.4 all-to-all-done.1
  67.6 14.7 %reshape.178 = bf16[12288,1,2,2]{3,2,1,0:T(2,128)(2,1)} reshape(bf16[4,2,6144]{2,1,0:T(2,128)(2,1)S(1)} %all-to-all-done.1) | data formatting | bytes 196608
  82.3 14.5 %copy.164 = bf16[1,2,2,4,3072]{4,3,2,1,0:T(4,128)(2,1)S(1)} copy(bf16[1,2,2,4,3072]{2,1,4,3,0:T(2,128)(2,1)} %bitcast.140) | data formatting | bytes 196608 | tf_op jit(solution)/shard_map/all_gather | solution.py:78
  96.8 16.5 %all_gather.15 = bf16[8,2,2,4,3072]{4,3,2,1,0:T(4,128)(2,1)S(1)} all-gather(bf16[1,2,2,4,3072]{4,3,2,1,0:T(4,128)(2,1)S(1)} %copy.164), channel_id=1, replica_groups=mesh['lat'=4,'kpt'=8] {'kpt'}, dimensions={0}, use_global_device_ids=true | all-gather | bytes 884736 | tf_op jit(solution)/shard_map/all_gather | solution.py:78
  115.1 1.4 fusion.2
  116.6 2.4 copy.137
  119.0 1.4 fusion.3
  120.4 2.6 %copy.140 = bf16[64,2,3072]{0,2,1:T(8,128)(2,1)} copy(bf16[64,2,3072]{2,0,1:T(8,128)(2,1)} %fusion.3) | data formatting | bytes 1572864 | tf_op jit(solution)/shard_map/convert.6
  123.0 10.7 %copy.142 = bf16[64,2,12,16,16]{4,3,2,1,0:T(8,128)(2,1)} copy(bf16[64,2,12,16,16]{0,4,3,2,1:T(8,128)(2,1)} %bitcast.142) | data formatting | bytes 1572864 | tf_op jit(solution)/shard_map/squeeze | solution.py:93
  133.7 9.8 %copy.139 = bf16[64,2,12,16,16]{4,3,2,1,0:T(8,128)(2,1)} copy(bf16[64,2,12,16,16]{0,4,3,2,1:T(8,128)(2,1)S(1)} %bitcast.141) | data formatting | bytes 1572864 | tf_op jit(solution)/shard_map/squeeze | solution.py:92
  143.5 9.2 %fusion.21 = f32[64,2,12,16,16]{4,3,2,1,0:T(8,128)} fusion(bf16[64,2,12,16,16]{4,3,2,1,0:T(8,128)(2,1)} %copy.139, bf16[1,64,16,16]{3,2,1,0:T(8,128)(2,1)S(1)} %copy-done.4), kind=kOutput, calls=%fused_computation.32 | convolution fusion | flops 12582912 | bytes 2392064 | tf_op jit(solution)/shard_map/kqmab,kbn->kqman/dot_general | solution.py:94
  152.7 5.5 %fusion.19 = f32[64,2,12,16,16]{4,3,2,1,0:T(8,128)} fusion(bf16[64,2,12,16,16]{4,3,2,1,0:T(8,128)(2,1)S(1)} %copy-done.1, bf16[1,64,16,16]{3,2,1,0:T(8,128)(2,1)S(1)} %copy-done.3), kind=kOutput, calls=%fused_computation.30 | convolution fusion | flops 12582912 | bytes 2392064 | tf_op jit(solution)/shard_map/kqmab,kbn->kqman/dot_general | solution.py:91
  158.2 8.2 %add_convert_fusion = bf16[64,2,12,16,16]{4,3,2,1,0:T(8,128)(2,1)S(1)} fusion(f32[64,2,12,16,16]{4,3,2,1,0:T(8,128)} %fusion.21, bf16[64,2,12,16,16]{4,3,2,1,0:T(8,128)(2,1)} %copy.142, bf16[1,64,16,16]{3,2,1,0:T(8,128)(2,1)S(1)} %copy-done.3), kind=kOutput, calls=%fused_computation.4 | convolution fusion | flops 13369344 | bytes 3178496 | tf_op jit(solution)/shard_map/kqmab,kbn->kqman/dot_general | solution.py:96
  166.4 10.9 %subtract_convert_fusion = bf16[64,2,12,16,16]{4,3,2,1,0:T(8,128)(2,1)} fusion(f32[64,2,12,16,16]{4,3,2,1,0:T(8,128)} %fusion.19, bf16[64,2,12,16,16]{4,3,2,1,0:T(8,128)(2,1)} %copy.142, bf16[1,64,16,16]{3,2,1,0:T(8,128)(2,1)S(1)} %copy-done.4), kind=kOutput, calls=%fused_computation.5 | convolution fusion | flops 13369344 | bytes 3178496 | tf_op jit(solution)/shard_map/kqmab,kbn->kqman/dot_general | solution.py:93
  177.3 9.6 %fusion.10 = f32[64,2,12,16,16]{4,3,2,1,0:T(8,128)} fusion(bf16[64,2,12,16,16]{4,3,2,1,0:T(8,128)(2,1)} %subtract_convert_fusion, bf16[1,2,64,16,16]{4,3,1,2,0:T(8,128)(2,1)S(1)} %copy.172), kind=kOutput, calls=%fused_computation.21 | convolution fusion | flops 12582912 | bytes 2424832 | tf_op jit(solution)/shard_map/qkac,kqman->kqmcn/dot_general | solution.py:104
  186.8 5.5 %fusion.16 = f32[64,2,12,16,16]{4,3,2,1,0:T(8,128)} fusion(bf16[64,2,12,16,16]{4,3,2,1,0:T(8,128)(2,1)S(1)} %copy-done, bf16[1,2,64,16,16]{4,3,1,2,0:T(8,128)(2,1)S(1)} %copy.171), kind=kOutput, calls=%fused_computation.27 | convolution fusion | flops 12582912 | bytes 2424832 | tf_op jit(solution)/shard_map/qkac,kqman->kqmcn/dot_general | solution.py:99
  192.3 5.5 %fusion.14 = f32[64,2,12,16,16]{4,3,2,1,0:T(8,128)} fusion(bf16[64,2,12,16,16]{4,3,2,1,0:T(8,128)(2,1)S(1)} %add_convert_fusion, bf16[1,2,64,16,16]{4,3,1,2,0:T(8,128)(2,1)S(1)} %copy.171), kind=kOutput, calls=%fused_computation.25 | convolution fusion | flops 12582912 | bytes 2424832 | tf_op jit(solution)/shard_map/qkac,kqman->kqmcn/dot_general | solution.py:102
  197.8 5.5 %fusion.12 = f32[64,2,12,16,16]{4,3,2,1,0:T(8,128)} fusion(bf16[64,2,12,16,16]{4,3,2,1,0:T(8,128)(2,1)S(1)} %add_convert_fusion, bf16[1,2,64,16,16]{4,3,1,2,0:T(8,128)(2,1)S(1)} %copy.172), kind=kOutput, calls=%fused_computation.23 | convolution fusion | flops 12582912 | bytes 2424832 | tf_op jit(solution)/shard_map/qkac,kqman->kqmcn/dot_general | solution.py:101
  203.3 9.7 %copy.154 = f32[64,2,12,16,16]{0,3,4,2,1:T(8,128)S(1)} copy(f32[64,2,12,16,16]{4,3,2,1,0:T(8,128)} %fusion.10) | data formatting | bytes 3145728 | tf_op jit(solution)/shard_map/qkac,kqman->kqmcn/dot_general | solution.py:104
  213.0 10.9 %copy.149 = f32[64,2,12,16,16]{0,3,4,2,1:T(8,128)} copy(f32[64,2,12,16,16]{4,3,2,1,0:T(8,128)} %fusion.16) | data formatting | bytes 3145728 | tf_op jit(solution)/shard_map/qkac,kqman->kqmcn/dot_general | solution.py:99
  223.9 10.9 %copy.153 = f32[64,2,12,16,16]{0,3,4,2,1:T(8,128)} copy(f32[64,2,12,16,16]{4,3,2,1,0:T(8,128)} %fusion.14) | data formatting | bytes 3145728 | tf_op jit(solution)/shard_map/qkac,kqman->kqmcn/dot_general | solution.py:102
  234.8 10.9 %copy.150 = f32[64,2,12,16,16]{0,3,4,2,1:T(8,128)} copy(f32[64,2,12,16,16]{4,3,2,1,0:T(8,128)} %fusion.12) | data formatting | bytes 3145728 | tf_op jit(solution)/shard_map/qkac,kqman->kqmcn/dot_general | solution.py:101
  245.7 5.0 %fusion.5 = (bf16[64,2,12,16,16]{0,4,3,2,1:T(8,128)(2,1)S(1)}, bf16[64,2,12,16,16]{0,4,3,2,1:T(8,128)(2,1)S(1)}) fusion(f32[64,2,12,16,16]{0,3,4,2,1:T(8,128)} %copy.149, f32[64,2,12,16,16]{0,3,4,2,1:T(8,128)} %copy.150, f32[64,2,16,16]{0,3,2,1:T(8,128)S(1)} %copy-done.5, f32[64,2,12,16,16]{0,3,4,2,1:T(8,128)} %copy.153, f32[64,2,12,16,16]{0,3,4,2,1:T(8,128)S(1)} %copy.154), kind=kLoop, calls=%fused_computation.14 | loop fusion | flops 2359296 | bytes 7995392 | tf_op jit(solution)/shard_map/convert.3
  250.8 0.7 pad_maximum_fusion
  251.5 3.3 %copy.155 = bf16[2,64,2,3072]{3,2,1,0:T(2,128)(2,1)} copy(bf16[2,64,2,3072]{1,3,2,0:T(8,128)(2,1)S(1)} %pad_maximum_fusion) | data formatting | bytes 3145728 | tf_op jit(solution)/shard_map/stack | solution.py:109
  (39 shorter events, 5.0 us)
Async XLA Ops:
  4.6 27.7 %all-to-all-start = ((bf16[2,1,4,12288]{3,0,1,2:T(2,128)(2,1)}), bf16[2,1,4,12288]{3,0,1,2:T(2,128)(2,1)S(1)}, u32[]{:S(2)}, u32[]{:S(2)}) async-start(bf16[2,1,4,12288]{3,0,1,2:T(2,128)(2,1)} %copy.130), calls=%async_computation | async-start | bytes 393216 | tf_op jit(solution)/shard_map/all_to_all | solution.py:73
  37.5 25.2 %copy-start.6 = (s32[32]{0:T(128)S(1)}, s32[32]{0:T(128)}, u32[]{:S(2)}) copy-start(s32[32]{0:T(128)} %param.16) | copy-start | bytes 388
  59.4 8.2 %all-to-all-start.1 = ((bf16[4,2,6144]{2,1,0:T(2,128)(2,1)}), bf16[4,2,6144]{2,1,0:T(2,128)(2,1)S(1)}, u32[]{:S(2)}, u32[]{:S(2)}) async-start(bf16[4,2,6144]{2,1,0:T(2,128)(2,1)} %reshape.177), calls=%async_computation.1 | async-start | bytes 196608 | tf_op jit(solution)/shard_map/all_to_all | solution.py:76
  120.4 13.3 %copy-start.2 = (bf16[64,2,3072]{0,2,1:T(8,128)(2,1)S(1)}, bf16[64,2,3072]{0,2,1:T(8,128)(2,1)}, u32[]{:S(2)}) copy-start(bf16[64,2,3072]{0,2,1:T(8,128)(2,1)} %copy.137) | copy-start | bytes 2359300
  123.0 20.5 %copy-start.4 = (bf16[1,64,16,16]{3,2,1,0:T(8,128)(2,1)S(1)}, bf16[1,64,16,16]{3,2,1,0:T(8,128)(2,1)}, u32[]{:S(2)}) copy-start(bf16[1,64,16,16]{3,2,1,0:T(8,128)(2,1)} %copy.170) | copy-start | bytes 98308
  143.5 9.2 %copy-start.1 = (bf16[64,2,12,16,16]{4,3,2,1,0:T(8,128)(2,1)S(1)}, bf16[64,2,12,16,16]{4,3,2,1,0:T(8,128)(2,1)}, u32[]{:S(2)}) copy-start(bf16[64,2,12,16,16]{4,3,2,1,0:T(8,128)(2,1)} %copy.139) | copy-start | bytes 2359300
  143.5 9.2 %copy-start.3 = (bf16[1,64,16,16]{3,2,1,0:T(8,128)(2,1)S(1)}, bf16[1,64,16,16]{3,2,1,0:T(8,128)(2,1)}, u32[]{:S(2)}) copy-start(bf16[1,64,16,16]{3,2,1,0:T(8,128)(2,1)} %copy.169) | copy-start | bytes 98308
  177.2 9.6 %copy-start = (bf16[64,2,12,16,16]{4,3,2,1,0:T(8,128)(2,1)S(1)}, bf16[64,2,12,16,16]{4,3,2,1,0:T(8,128)(2,1)}, u32[]{:S(2)}) copy-start(bf16[64,2,12,16,16]{4,3,2,1,0:T(8,128)(2,1)} %subtract_convert_fusion) | copy-start | bytes 2359300
  234.8 10.9 %copy-start.5 = (f32[64,2,16,16]{0,3,2,1:T(8,128)S(1)}, f32[64,2,16,16]{0,3,2,1:T(8,128)}, u32[]{:S(2)}) copy-start(f32[64,2,16,16]{0,3,2,1:T(8,128)} %broadcast_multiply_fusion) | copy-start | bytes 393220
